TPU v7x, 256 devices: a whole 4x4x8 slice. The times are simulated.
256 devices in a mesh: row: 8 (over x, core), col: 32 (over y, z).
Axes of the slice: x: 4, y: 4, z: 8, core: 2. Of those that a mesh axis runs over, the one named last changes fastest.
Arguments:
- affinity_tiles: bfloat16 [1024, 64, 128, 128], P(('row', 'col'))
- block_columns: int32 [1024, 64], P(('row', 'col')), may hold values from 0 to 127, as said below
- live_counts: int32 [8, 128], P('row', 'col'), may hold values from 1 to 64, 4096 in all within a row
- earlier_blocks: float32 [4, 64, 131072], P(None, None, ('row', 'col')), may hold values from -6 to 6
Outputs:
- new_blocks: float32 [2, 64, 131072], P(None, None, ('row', 'col'))
- triangular_factors: float32 [2, 64, 64], replicated
Inputs may be any that keep to these rules, and one draw needn't show every extreme that they name: `block_columns`: slot 0 of every block row names the block row itself; columns name block rows of the same row group. `live_counts`: slots at or past a block row's count are ignored.
All inputs are finite; a program needn't handle non-finite values.
Results may differ from a plain program's by a relative error of at most 0.0059.
Values may be sent and summed in bfloat16 or wider, within the bound.
No kernel may reach another device: no remote copies, remote signals or barrier semaphores. Data moves between devices by JAX's collectives and lax.ppermute only.
A program may use at most 64 MiB of HBM per device.

v0:
```python
import jax
import jax.numpy as jnp
from jax import lax
from jax.sharding import PartitionSpec as P

STEPS = 2


def apply_tiles(affinity_tiles, block_columns, row_counts, group_blocks):
    block_rows = affinity_tiles.shape[0]
    slot_count = affinity_tiles.shape[1]
    tile_size = affinity_tiles.shape[2]
    block_width = group_blocks.shape[0]
    slot_ids = lax.broadcasted_iota(jnp.int32, (block_rows, slot_count), 1)
    live_mask = slot_ids < row_counts[:, None]
    picked = jnp.take(group_blocks, block_columns, axis=1)
    picked = jnp.where(live_mask[None, :, :, None], picked, jnp.zeros((), jnp.bfloat16))
    running = jnp.einsum(
        "rsij,brsj->bri", affinity_tiles, picked, preferred_element_type=jnp.float32
    )
    return running.reshape(block_width, block_rows * tile_size)


def on_device(affinity_tiles, block_columns, live_counts, earlier_blocks):
    block_rows = affinity_tiles.shape[0]
    tile_size = affinity_tiles.shape[2]
    block_width = earlier_blocks.shape[1]
    rows_here = earlier_blocks.shape[2]
    total_rows = rows_here * lax.axis_size("row") * lax.axis_size("col")
    row_counts = live_counts.reshape(block_rows)
    known_list = [earlier_blocks[i] for i in range(earlier_blocks.shape[0])]
    first_half = known_list[-1].astype(jnp.bfloat16)
    group_half = lax.all_gather(first_half, "col", axis=1, tiled=True)
    fresh_list = []
    factor_list = []
    for step_index in range(STEPS):
        is_last = step_index + 1 == STEPS
        group_blocks = group_half.reshape(block_width, -1, tile_size)
        product = apply_tiles(affinity_tiles, block_columns, row_counts, group_blocks)
        known = jnp.concatenate(known_list, 0)
        local_proj = jnp.dot(known, product.T, precision=lax.Precision.HIGHEST) / total_rows
        projections = lax.psum(local_proj, ("row", "col"))
        residual = product - jnp.dot(projections.T, known, precision=lax.Precision.HIGHEST)
        local_gram = jnp.dot(residual, residual.T, precision=lax.Precision.HIGHEST) / total_rows
        gram_sum = lax.psum(local_gram, ("row", "col"))
        factor_low = jnp.linalg.cholesky(gram_sum)
        fresh = jax.scipy.linalg.solve_triangular(factor_low, residual, lower=True)
        fresh_list.append(fresh)
        factor_list.append(factor_low.T)
        known_list.append(fresh)
        if not is_last:
            group_half = lax.all_gather(fresh.astype(jnp.bfloat16), "col", axis=1, tiled=True)
    return (jnp.stack(fresh_list), jnp.stack(factor_list))


def solution(mesh):
    return jax.shard_map(
        on_device,
        mesh=mesh,
        in_specs=(
            P(("row", "col"), None, None, None),
            P(("row", "col"), None),
            P("row", "col"),
            P(None, None, ("row", "col")),
        ),
        out_specs=(P(None, None, ("row", "col")), P()),
        check_vma=False,
    )
```

profile of v0, /device:TPU:1, one launch (start us, length us, event | category | flops | bytes accessed | tf_op | source)
XLA Modules:
  0.0 864.7 jit_solution(17645085274301516106)
XLA Ops:
  7.2 1.5 fusion.32
  11.3 0.9 constant_dynamic-update-slice_fusion.3
  13.1 1.1 slice_bitcast_fusion.2
  14.3 71.6 %all-gather.3.cloned.1.call-done = bf16[64,16384]{1,0:T(8,128)(2,1)} async-done(((bf16[64,512]{1,0:T(8,128)(2,1)}), bf16[64,16384]{1,0:T(8,128)(2,1)}) %all-gather.3.cloned.1.call-update) | async-done | bytes 2097168 | tf_op jit(solution)/shard_map/all_gather | solution.py:33
  85.9 2.2 copy_bitcast_fusion.1
  88.1 3.0 gather_fusion
  91.1 6.3 fusion.12
  97.3 1.2 convolution_multiply_fusion.1
  99.6 246.5 %all-reduce.3.cloned.1.call-done = f32[256,64]{1,0:T(8,128)} async-done(((f32[256,64]{1,0:T(8,128)}), f32[256,64]{1,0:T(8,128)}) %all-reduce.3.cloned.1.call-update) | async-done | bytes 65552 | tf_op jit(solution)/shard_map/psum | solution.py:42
  346.0 1.3 convolution_subtract_fusion.1
  347.6 76.2 %psum.29 = f32[64,64]{0,1:T(8,128)S(1)} all-reduce(f32[64,64]{0,1:T(8,128)S(1)} %convolution_multiply_fusion.3), channel_id=1, replica_groups=mesh['row'=8,'col'=32] {'row','col'}, use_global_device_ids=true, to_apply=%region_1.3 | all-reduce | flops 4096 | bytes 32768 | tf_op jit(solution)/shard_map/psum | solution.py:45
  423.9 5.8 cholesky.44
  431.1 4.9 custom-call.6
  436.0 1.0 fusion.33
  437.0 66.8 %all-gather.5.cloned.1.call-done = bf16[64,16384]{1,0:T(8,128)(2,1)} async-done(((bf16[64,512]{1,0:T(8,128)(2,1)}), bf16[64,16384]{1,0:T(8,128)(2,1)}) %all-gather.5.cloned.1.call-update) | async-done | bytes 2097168 | tf_op jit(solution)/shard_map/all_gather | solution.py:52
  503.8 2.2 copy_bitcast_fusion
  506.0 3.0 gather_fusion.1
  509.0 6.3 fusion.13
  515.3 1.3 convolution_multiply_fusion
  516.7 251.0 %all-reduce.5.cloned.1.call-done = f32[320,64]{1,0:T(8,128)} async-done(((f32[320,64]{1,0:T(8,128)}), f32[320,64]{1,0:T(8,128)}) %all-reduce.5.cloned.1.call-update) | async-done | bytes 81936 | tf_op jit(solution)/shard_map/psum | solution.py:42
  767.7 1.5 convolution_subtract_fusion
  769.4 74.8 %psum.31 = f32[64,64]{0,1:T(8,128)S(1)} all-reduce(f32[64,64]{0,1:T(8,128)S(1)} %convolution_multiply_fusion.2), channel_id=1, replica_groups=mesh['row'=8,'col'=32] {'row','col'}, use_global_device_ids=true, to_apply=%region_5.9 | all-reduce | flops 4096 | bytes 32768 | tf_op jit(solution)/shard_map/psum | solution.py:45
  844.3 5.8 cholesky.55
  852.2 4.9 custom-call.7
  (31 shorter events, 9.6 us)
Async XLA Ops:
  7.2 78.7 %all-gather.3.cloned.1.call-start = ((), (), s32[]{:S(2)}) async-start(), calls=%async_computation | async-start | bytes 2162688 | tf_op jit(solution)/shard_map/all_gather | solution.py:33
  8.8 337.2 %all-reduce.3.cloned.1.call-start = ((), (), s32[]{:S(2)}) async-start(), calls=%async_computation.1 | async-start | bytes 262144 | tf_op jit(solution)/shard_map/psum | solution.py:42
  98.6 405.2 %all-gather.5.cloned.1.call-start = ((), (), s32[]{:S(2)}) async-start(), calls=%async_computation.2 | async-start | bytes 2162688 | tf_op jit(solution)/shard_map/all_gather | solution.py:52
  437.0 330.7 %all-reduce.5.cloned.1.call-start = ((), (), s32[]{:S(2)}) async-start(), calls=%async_computation.3 | async-start | bytes 327680 | tf_op jit(solution)/shard_map/psum | solution.py:42
Sparse Core Ops, SparseCore 0:
  11.0 74.8 all-gather.2
  98.7 247.2 all-reduce.2
  437.1 66.6 all-gather.4
  516.8 250.8 all-reduce.4
where the time goes:
time: 865 us
  waiting for transfers between devices  636 us (74%)
  blocking collectives  151 us (17%)
  other arithmetic  26.4 us (3%)
  matrix products  19.7 us (2%)
  local copies, waits for them, and re-layouts  17.7 us (2%)
  between operations  13.9 us (2%)
    psum x2, waiting for transfers between devices, on_device(): projections = lax.psum(local_proj, ('row', 'col'))  497 us
    psum x2, blocking collectives, on_device(): gram_sum = lax.psum(local_gram, ('row', 'col'))  151 us
    all_gather x1, waiting for transfers between devices, on_device(): group_half = lax.all_gather(first_half, 'col', axis=1, tiled=True)  71.6 us
    all_gather x1, waiting for transfers between devices, on_device(): lax.all_gather(fresh.astype(jnp.bfloat16), 'col', axis=1, tiled=True)  66.8 us
  transfers between devices with their start and end apart: 4, of which 4 were waited for; matrix products, arithmetic and copies ran while one was open for 1% of the time, Pallas kernels for 0%

commit v1 on v0

--- a/solution.py
+++ b/solution.py
@@ -30,7 +30,9 @@
     row_counts = live_counts.reshape(block_rows)
     known_list = [earlier_blocks[i] for i in range(earlier_blocks.shape[0])]
     first_half = known_list[-1].astype(jnp.bfloat16)
-    group_half = lax.all_gather(first_half, "col", axis=1, tiled=True)
+    group_half = jnp.concatenate(
+        lax.all_to_all(jnp.stack([first_half] * lax.axis_size("col")), "col", 0, 0), axis=1
+    )
     fresh_list = []
     factor_list = []
     for step_index in range(STEPS):

time: 865 us -> 845 us (0.977)
  waiting for transfers between devices: 636 us -> 602 us
  starting transfers between devices: 0.16 us -> 12.3 us
    all_gather x1 -> x0, waiting for transfers between devices: 71.6 us -> none  [on_device(): group_half = lax.all_gather(first_half, 'col', axis=1, tiled=True)]
    all_to_all x0 -> x1, waiting for transfers between devices: none -> 47.9 us  [on_device(): lax.all_to_all(jnp.stack([first_half] * lax.axis_size('col')), 'col', 0, 0)]
    all_to_all x0 -> x1, starting transfers between devices: none -> 12 us  [on_device(): lax.all_to_all(jnp.stack([first_half] * lax.axis_size('col')), 'col', 0, 0)]
    another operation x0 -> x4, local copies, waits for them, and re-layouts: none -> 9.86 us  [the longest x2 7.3 us: on_device(): group_blocks = group_half.reshape(block_width, -1, tile_size)]
    psum x2, waiting for transfers between devices: 497 us -> 488 us  [on_device(): projections = lax.psum(local_proj, ('row', 'col'))]
  transfers between devices with their start and end apart: 4 -> 4, of which waited for: 4 -> 4; matrix products, arithmetic and copies ran while one was open for 1% -> 0% of each run, Pallas kernels for 0% -> 0%
where the time goes in v1:
time: 845 us; the launch traced here: 844 us
  waiting for transfers between devices  602 us (71%)
  blocking collectives  149 us (18%)
  other arithmetic  25 us (3%)
  local copies, waits for them, and re-layouts  22.3 us (3%)
  matrix products  19.7 us (2%)
  between operations  14 us (2%)
  starting transfers between devices  12.3 us (1%)
    psum x2, waiting for transfers between devices, on_device(): projections = lax.psum(local_proj, ('row', 'col'))  488 us
    psum x2, blocking collectives, on_device(): gram_sum = lax.psum(local_gram, ('row', 'col'))  149 us
    all_gather x1, waiting for transfers between devices, on_device(): lax.all_gather(fresh.astype(jnp.bfloat16), 'col', axis=1, tiled=True)  65.5 us
    all_to_all x1, waiting for transfers between devices, on_device(): lax.all_to_all(jnp.stack([first_half] * lax.axis_size('col')), 'col', 0, 0)  47.9 us
  transfers between devices with their start and end apart: 4, of which 4 were waited for; matrix products, arithmetic and copies ran while one was open for 0% of the time, Pallas kernels for 0%

profile of v1, /device:TPU:1, one launch (start us, length us, event | category | flops | bytes accessed | tf_op | source)
XLA Modules:
  0.0 844.0 jit_solution(10965521268150021920)
XLA Ops:
  8.2 1.6 stack.17
  9.8 12.0 %all-to-all-start = ((bf16[32,64,512]{2,1,0:T(8,128)(2,1)}), bf16[32,64,512]{2,1,0:T(8,128)(2,1)S(1)}, u32[]{:S(2)}, u32[]{:S(2)}) async-start(bf16[32,64,512]{2,1,0:T(8,128)(2,1)} %stack.17), calls=%async_computation | async-start | bytes 4194304 | tf_op jit(solution)/shard_map/all_to_all | solution.py:34
  22.8 47.9 %all-to-all-done = bf16[32,64,512]{2,1,0:T(8,128)(2,1)S(1)} async-done(((bf16[32,64,512]{2,1,0:T(8,128)(2,1)}), bf16[32,64,512]{2,1,0:T(8,128)(2,1)S(1)}, u32[]{:S(2)}, u32[]{:S(2)}) %all-to-all-start) | async-done | bytes 2097184 | tf_op jit(solution)/shard_map/all_to_all | solution.py:34
  70.7 2.5 copy.21
  73.2 4.4 reshape_reshape.3
  77.6 2.9 copy.22
  80.5 3.0 gather_fusion
  83.5 6.3 fusion.12
  89.8 1.2 convolution_multiply_fusion.1
  91.2 240.9 %all-reduce.3.cloned.1.call-done = f32[256,64]{0,1:T(8,128)} async-done(((f32[256,64]{0,1:T(8,128)}), f32[256,64]{0,1:T(8,128)}) %all-reduce.3.cloned.1.call-update) | async-done | bytes 65552 | tf_op jit(solution)/shard_map/psum | solution.py:44
  332.1 1.3 convolution_subtract_fusion.1
  333.6 74.7 %psum.29 = f32[64,64]{0,1:T(8,128)S(1)} all-reduce(f32[64,64]{0,1:T(8,128)S(1)} %convolution_multiply_fusion.3), channel_id=1, replica_groups=mesh['row'=8,'col'=32] {'row','col'}, use_global_device_ids=true, to_apply=%region_1.3 | all-reduce | flops 4096 | bytes 32768 | tf_op jit(solution)/shard_map/psum | solution.py:47
  408.4 5.8 cholesky.44
  415.6 4.9 custom-call.6
  421.7 65.5 %all-gather.2.cloned.1.call-done = bf16[64,16384]{1,0:T(8,128)(2,1)} async-done(((bf16[64,512]{1,0:T(8,128)(2,1)}), bf16[64,16384]{1,0:T(8,128)(2,1)}) %all-gather.2.cloned.1.call-update) | async-done | bytes 2097168 | tf_op jit(solution)/shard_map/all_gather | solution.py:54
  487.2 2.2 copy_bitcast_fusion
  489.3 3.0 gather_fusion.1
  492.4 6.3 fusion.13
  498.6 1.4 convolution_multiply_fusion
  500.0 247.4 %all-reduce.5.cloned.1.call-done = f32[320,64]{0,1:T(8,128)} async-done(((f32[320,64]{0,1:T(8,128)}), f32[320,64]{0,1:T(8,128)}) %all-reduce.5.cloned.1.call-update) | async-done | bytes 81936 | tf_op jit(solution)/shard_map/psum | solution.py:44
  747.4 1.4 convolution_subtract_fusion
  749.1 74.4 %psum.31 = f32[64,64]{0,1:T(8,128)S(1)} all-reduce(f32[64,64]{0,1:T(8,128)S(1)} %convolution_multiply_fusion.2), channel_id=1, replica_groups=mesh['row'=8,'col'=32] {'row','col'}, use_global_device_ids=true, to_apply=%region_5.9 | all-reduce | flops 4096 | bytes 32768 | tf_op jit(solution)/shard_map/psum | solution.py:47
  823.6 5.8 cholesky.55
  831.5 4.9 custom-call.7
  (43 shorter events, 8.4 us)
Async XLA Ops:
  7.2 14.9 %copy-start = (f32[4,64,512]{2,1,0:T(8,128)S(1)}, f32[4,64,512]{2,1,0:T(8,128)}, u32[]{:S(2)}) copy-start(f32[4,64,512]{2,1,0:T(8,128)} %param.12) | copy-start | bytes 1572868
  7.2 14.7 %copy-start.3 = (s32[4,64]{1,0:T(4,128)S(1)}, s32[4,64]{1,0:T(4,128)}, u32[]{:S(2)}) copy-start(s32[4,64]{1,0:T(4,128)} %param.10) | copy-start | bytes 3076
  7.2 14.8 %copy-start.4 = (s32[1,4]{1,0:T(1,128)S(1)}, s32[1,4]{1,0:T(1,128)}, u32[]{:S(2)}) copy-start(s32[1,4]{1,0:T(1,128)} %param.11) | copy-start | bytes 52
  9.8 60.9 %all-to-all-start = ((bf16[32,64,512]{2,1,0:T(8,128)(2,1)}), bf16[32,64,512]{2,1,0:T(8,128)(2,1)S(1)}, u32[]{:S(2)}, u32[]{:S(2)}) async-start(bf16[32,64,512]{2,1,0:T(8,128)(2,1)} %stack.17), calls=%async_computation | async-start | bytes 4194304 | tf_op jit(solution)/shard_map/all_to_all | solution.py:34
  21.8 310.3 %all-reduce.3.cloned.1.call-start = ((), (), s32[]{:S(2)}) async-start(), calls=%async_computation.1 | async-start | bytes 131072 | tf_op jit(solution)/shard_map/psum | solution.py:44
  83.5 6.3 copy-start.1
  83.5 6.3 copy-start.2
  91.1 396.0 %all-gather.2.cloned.1.call-start = ((), (), s32[]{:S(2)}) async-start(), calls=%async_computation.2 | async-start | bytes 2162688 | tf_op jit(solution)/shard_map/all_gather | solution.py:54
  421.5 325.9 %all-reduce.5.cloned.1.call-start = ((), (), s32[]{:S(2)}) async-start(), calls=%async_computation.3 | async-start | bytes 196608 | tf_op jit(solution)/shard_map/psum | solution.py:44
Sparse Core Ops, SparseCore 0:
  91.2 240.8 all-reduce.2
  421.6 65.5 all-gather.1
  500.1 247.2 all-reduce.4
